TPU v7x, 256 devices: a whole 4x4x8 slice. The times are simulated.
256 devices in a mesh: wide: 16 (over z_hi, x, core), col: 16 (over y, z_lo).
Axes of the slice: x: 4, y: 4, z: 8 (z_hi: 2, z_lo: 4; z = z_hi * 4 + z_lo), core: 2. Of those that a mesh axis runs over, the one named last changes fastest.
Arguments:
- adjoint: bfloat16 [32, 6144], P(None, ('wide', 'col')), may hold values from -6 to 6
- operator: bfloat16 [6144, 196608], P('wide', 'col'), may hold values from -0.109375 to 0.109375
- owner: int32 [196608], P(('col', 'wide')), may hold values from 0 to 196607, as said below
Outputs:
- junction_sums: float32 [32, 196608], P(None, ('col', 'wide'))
Inputs may be any that keep to these rules, and one draw needn't show every extreme that they name: Unknown j of device block b = j // 768 (blocks ordered col first, then wide) has owner j itself, or is a duplicate whose owner is an unknown in the lower half of a block of the same index of col; duplicates lie only in the upper half of a block and owners of duplicates are never duplicates. One block hands at most 16 duplicates to the blocks of any one index of wide, and this count is reached in every draw, by some block towards every index of wide and towards some index of wide from every block.
All inputs are finite; a program needn't handle non-finite values.
Results may differ from a plain program's by a relative error of at most 0.0003.
Values may be sent and summed in bfloat16 or wider, within the bound.
No kernel may reach another device: no remote copies, remote signals or barrier semaphores. Data moves between devices by JAX's collectives and lax.ppermute only.
A program may use at most 64 MiB of HBM per device.

v0:
```python
import jax
import jax.numpy as jnp
from jax import lax
from jax.sharding import PartitionSpec as P

CAP = 16


def local(adjoint, operator, owner):
    wide_count = lax.axis_size("wide")
    own_width = owner.shape[0]
    block_cols = operator.shape[1]
    sensors = adjoint.shape[0]
    partials = jnp.dot(
        lax.all_gather(adjoint, "col", axis=1, tiled=True),
        operator,
        preferred_element_type=jnp.float32,
    )
    col_base = lax.axis_index("col") * block_cols
    summed = lax.psum_scatter(partials, "wide", scatter_dimension=1, tiled=True)
    positions = jnp.arange(own_width, dtype=jnp.int32)
    global_cols = col_base + lax.axis_index("wide") * own_width + positions
    repeated = owner != global_cols
    target_peer = owner // own_width % wide_count
    target_place = owner % own_width
    peers = jnp.arange(wide_count, dtype=jnp.int32)
    marks = ((target_peer[:, None] == peers[None, :]) & repeated[:, None]).astype(jnp.int32)
    ranking = jnp.sum((jnp.cumsum(marks, axis=0) - marks) * marks, axis=1)
    slot_of = target_peer * CAP + ranking
    slot_ids = jnp.arange(wide_count * CAP, dtype=jnp.int32)
    chosen = (slot_of[:, None] == slot_ids[None, :]) & repeated[:, None]
    selector = chosen.astype(jnp.float32)
    outgoing = jnp.dot(
        summed, selector, precision=lax.Precision.HIGHEST, preferred_element_type=jnp.float32
    )
    place_sum = jnp.sum(chosen.astype(jnp.int32) * (target_place + 1)[:, None], axis=0) - 1
    outgoing = outgoing.reshape(sensors, wide_count, CAP)
    places = place_sum.astype(jnp.float32).reshape(1, wide_count, CAP)
    arrived, arrived_places = (
        lax.all_to_all(outgoing, "wide", split_axis=1, concat_axis=1, tiled=True),
        lax.all_to_all(places, "wide", split_axis=1, concat_axis=1, tiled=True),
    )
    flat_values = arrived.reshape(sensors, wide_count * CAP)
    landing = arrived_places.reshape(-1).astype(jnp.int32)
    receiver = (landing[:, None] == positions[None, :]).astype(jnp.float32)
    kept = summed * (1.0 - repeated.astype(jnp.float32))[None, :]
    added = jnp.dot(
        flat_values, receiver, precision=lax.Precision.HIGHEST, preferred_element_type=jnp.float32
    )
    return kept + added


def solution(mesh):
    return jax.shard_map(
        local,
        mesh=mesh,
        in_specs=(P(None, ("wide", "col")), P("wide", "col"), P(("col", "wide"))),
        out_specs=P(None, ("col", "wide")),
        check_vma=False,
    )
```

profile of v0, /device:TPU:1, one launch (start us, length us, event | category | flops | bytes accessed | tf_op | source)
XLA Modules:
  0.0 167.5 jit_solution(11518465624353053526)
XLA Ops:
  6.5 0.0 copy-start
  6.5 0.0 reduce-scatter.2.cloned.1.call-start
  6.5 38.5 %all_gather.3 = bf16[32,384]{0,1:T(8,128)(2,1)S(1)} all-gather(bf16[32,24]{0,1:T(8,128)(2,1)} %param.3), channel_id=1, replica_groups=mesh['wide'=16,'col'=16] {'col'}, dimensions={1}, use_global_device_ids=true | all-gather | bytes 26112 | tf_op jit(solution)/shard_map/all_gather | solution.py:15
  45.0 6.5 %fusion.15 = f32[32,12288]{1,0:T(8,128)} fusion(bf16[32,384]{0,1:T(8,128)(2,1)S(1)} %all_gather.3, bf16[384,12288]{1,0:T(8,128)(2,1)} %param.4), kind=kOutput, calls=%fused_computation.35 | convolution fusion | flops 301989888 | bytes 11034624 | tf_op jit(solution)/shard_map/dot_general | solution.py:14
  51.5 0.0 reduce-scatter.2.cloned.1.call-update
  51.5 0.0 copy-done
  51.6 1.7 %reduce-window.6 = s32[16,6,128]{2,0,1:T(8,128)S(1)} reduce-window(s32[16,6,128]{2,0,1:T(8,128)S(1)} %fusion.11, s32[]{:T(128)} %constant.48.clone.1), window={size=1x1x128 pad=0_0x0_0x127_0}, to_apply=%region_1.2 | reduce-window | flops 1560576 | bytes 98308 | tf_op jit(solution)/shard_map/reduce-window
  53.3 0.3 slice_reduce_fusion
  53.6 0.1 fusion.8
  53.7 0.7 select_reduce_fusion
  54.4 0.7 convert_element_type.40
  55.1 16.2 %all-to-all-start.1 = ((f32[1,16,16]{2,0,1:T(1,128)}), f32[1,16,16]{2,0,1:T(1,128)S(1)}, u32[]{:S(2)}, u32[]{:S(2)}) async-start(f32[1,16,16]{2,0,1:T(1,128)} %convert_element_type.40), calls=%async_computation.2 | async-start | bytes 16384 | tf_op jit(solution)/shard_map/all_to_all | solution.py:41
  71.2 67.5 %reduce-scatter.2.cloned.1.call-done = f32[32,768]{1,0:T(8,128)} async-done(((f32[32,12288]{1,0:T(8,128)}), f32[32,768]{1,0:T(8,128)}) %reduce-scatter.2.cloned.1.call-update) | async-done | bytes 98320 | tf_op jit(solution)/shard_map/reduce_scatter | solution.py:20
  138.8 1.9 %fusion.1 = f32[32,256]{0,1:T(8,128)S(1)} fusion(f32[32,768]{1,0:T(8,128)} %reduce-scatter.2.cloned.1.call-done, s32[768]{0:T(1024)S(1)} %multiply_add_fusion, pred[768]{0:T(1024)(128)(4,1)S(1)} %get-tuple-element.6), kind=kOutput, calls=%fused_computation.5 | convolution fusion | flops 75890688 | bytes 134912 | tf_op jit(solution)/shard_map/dot_general | solution.py:33
  140.7 0.7 reshape.65
  141.4 0.0 all-to-all-done.1
  141.4 6.2 %all-to-all-start = ((f32[16,1,512]{2,1,0:T(1,128)}), f32[16,1,512]{2,1,0:T(1,128)S(1)}, u32[]{:S(2)}, u32[]{:S(2)}) async-start(f32[16,1,512]{2,1,0:T(1,128)} %reshape.65), calls=%async_computation.1 | async-start | bytes 65536 | tf_op jit(solution)/shard_map/all_to_all | solution.py:40
  147.6 0.1 convert_element_type.42
  147.7 9.6 %all-to-all-done = f32[16,1,512]{2,1,0:T(1,128)S(1)} async-done(((f32[16,1,512]{2,1,0:T(1,128)}), f32[16,1,512]{2,1,0:T(1,128)S(1)}, u32[]{:S(2)}, u32[]{:S(2)}) %all-to-all-start) | async-done | bytes 32800 | tf_op jit(solution)/shard_map/all_to_all | solution.py:40
  157.3 0.5 broadcast.60
  157.8 0.7 reduce.6
  158.6 0.1 reshape.66
  158.6 2.0 %convolution_add_fusion = f32[32,768]{1,0:T(8,128)} fusion(f32[32,256]{0,1:T(8,128)S(1)} %bitcast.30, s32[256]{0:T(256)S(1)} %convert_element_type.42, f32[32,768]{1,0:T(8,128)} %reduce-scatter.2.cloned.1.call-done, f32[768]{0:T(1024)S(1)} %get-tuple-element.5), kind=kOutput, calls=%fused_computation | convolution fusion | flops 75743232 | bytes 233472 | tf_op jit(solution)/shard_map/dot_general | solution.py:47
  (7 shorter events, 0.1 us)
Async XLA Ops:
  6.5 45.0 %copy-start = (s32[768]{0:T(1024)S(1)}, s32[768]{0:T(1024)}, u32[]{:S(2)}) copy-start(s32[768]{0:T(1024)} %param.5) | copy-start | bytes 9220
  6.5 132.2 %reduce-scatter.2.cloned.1.call-start = ((), (), s32[]{:S(2)}) async-start(), calls=%async_computation.3 | async-start | bytes 1671168 | tf_op jit(solution)/shard_map/reduce_scatter | solution.py:20
  55.1 86.3 %all-to-all-start.1 = ((f32[1,16,16]{2,0,1:T(1,128)}), f32[1,16,16]{2,0,1:T(1,128)S(1)}, u32[]{:S(2)}, u32[]{:S(2)}) async-start(f32[1,16,16]{2,0,1:T(1,128)} %convert_element_type.40), calls=%async_computation.2 | async-start | bytes 16384 | tf_op jit(solution)/shard_map/all_to_all | solution.py:41
  141.4 15.9 %all-to-all-start = ((f32[16,1,512]{2,1,0:T(1,128)}), f32[16,1,512]{2,1,0:T(1,128)S(1)}, u32[]{:S(2)}, u32[]{:S(2)}) async-start(f32[16,1,512]{2,1,0:T(1,128)} %reshape.65), calls=%async_computation.1 | async-start | bytes 65536 | tf_op jit(solution)/shard_map/all_to_all | solution.py:40
Sparse Core Ops, SparseCore 0:
  51.6 87.0 reduce-scatter.1
where the time goes:
time: 168 us; the launch traced here: 167 us
  waiting for transfers between devices  77.2 us (46%)
  blocking collectives  38.5 us (23%)
  starting transfers between devices  22.3 us (13%)
  between operations  13.5 us (8%)
  matrix products  10.4 us (6%)
  other arithmetic  3.3 us (2%)
  local copies, waits for them, and re-layouts  2.36 us (1%)
    reduce_scatter x1, waiting for transfers between devices, local(): summed = lax.psum_scatter(partials, 'wide', scatter_dimension=1, tiled=True)  67.5 us
    all_gather x1, blocking collectives, local(): lax.all_gather(adjoint, 'col', axis=1, tiled=True)  38.5 us
    all_to_all x1, starting transfers between devices, local(): lax.all_to_all(places, 'wide', split_axis=1, concat_axis=1, tiled=True)  16.2 us
    all_to_all x1, waiting for transfers between devices, local(): lax.all_to_all(outgoing, 'wide', split_axis=1, concat_axis=1, tiled=True)  9.6 us
    dot_general x1, matrix products, local(): jnp.dot(lax.all_gather(adjoint, 'col', axis=1, tiled=True), operator, pre...  6.5 us
    all_to_all x1, starting transfers between devices, local(): lax.all_to_all(outgoing, 'wide', split_axis=1, concat_axis=1, tiled=True)  6.19 us
  transfers between devices with their start and end apart: 3, of which 2 were waited for; matrix products, arithmetic and copies ran while one was open for 4% of the time, Pallas kernels for 0%

commit v1 on v0

--- a/solution.py
+++ b/solution.py
@@ -12,7 +12,9 @@
     block_cols = operator.shape[1]
     sensors = adjoint.shape[0]
     partials = jnp.dot(
-        lax.all_gather(adjoint, "col", axis=1, tiled=True),
+        jnp.concatenate(
+            lax.all_to_all(jnp.stack([adjoint] * lax.axis_size("col")), "col", 0, 0), axis=1
+        ),
         operator,
         preferred_element_type=jnp.float32,
     )

time: 168 us -> 141 us (0.84)
  blocking collectives: 38.5 us -> 15.8 us
  starting transfers between devices: 22.3 us -> 16.5 us
    all_gather x1 -> x0, blocking collectives: 38.5 us -> none  [local(): lax.all_gather(adjoint, 'col', axis=1, tiled=True)]
    all_to_all x0 -> x1, blocking collectives: none -> 15.8 us  [local(): lax.all_to_all(jnp.stack([adjoint] * lax.axis_size('col')), 'col', 0, 0)]
    all_to_all x1, starting transfers between devices: 16.2 us -> 10.3 us  [local(): lax.all_to_all(places, 'wide', split_axis=1, concat_axis=1, tiled=True)]
where the time goes in v1:
time: 141 us
  waiting for transfers between devices  77.8 us (55%)
  starting transfers between devices  16.5 us (12%)
  blocking collectives  15.8 us (11%)
  between operations  13.5 us (10%)
  matrix products  10.4 us (7%)
  local copies, waits for them, and re-layouts  3.3 us (2%)
  other arithmetic  3.3 us (2%)
    reduce_scatter x1, waiting for transfers between devices, local(): summed = lax.psum_scatter(partials, 'wide', scatter_dimension=1, tiled=True)  68.2 us
    all_to_all x1, blocking collectives, local(): lax.all_to_all(jnp.stack([adjoint] * lax.axis_size('col')), 'col', 0, 0)  15.8 us
    all_to_all x1, starting transfers between devices, local(): lax.all_to_all(places, 'wide', split_axis=1, concat_axis=1, tiled=True)  10.3 us
    all_to_all x1, waiting for transfers between devices, local(): lax.all_to_all(outgoing, 'wide', split_axis=1, concat_axis=1, tiled=True)  9.6 us
    dot_general x1, matrix products, local(): jnp.dot(jnp.concatenate(lax.all_to_all(jnp.stack([adjoint] * lax.axis_siz...  6.5 us
    all_to_all x1, starting transfers between devices, local(): lax.all_to_all(outgoing, 'wide', split_axis=1, concat_axis=1, tiled=True)  6.15 us
  transfers between devices with their start and end apart: 3, of which 2 were waited for; matrix products, arithmetic and copies ran while one was open for 4% of the time, Pallas kernels for 0%

profile of v1, /device:TPU:1, one launch (start us, length us, event | category | flops | bytes accessed | tf_op | source)
XLA Modules:
  0.0 140.5 jit_solution(10042441039687070057)
XLA Ops:
  6.5 0.0 copy-start
  6.5 0.0 copy-start.1
  6.5 0.0 reduce-scatter.2.cloned.1.call-start
  6.5 0.7 copy-done
  7.2 0.1 reshape.75
  7.4 15.8 %all_to_all.15 = bf16[16,2,384]{2,1,0:T(2,128)(2,1)S(1)} all-to-all(bf16[16,2,384]{2,1,0:T(2,128)(2,1)S(1)} %reshape.75), channel_id=1, replica_groups=mesh['wide'=16,'col'=16] {'col'}, dimensions={0} | all-to-all | bytes 49152 | tf_op jit(solution)/shard_map/all_to_all | solution.py:16
  23.2 0.1 reshape.76
  23.3 6.5 %fusion.15 = f32[32,12288]{1,0:T(8,128)} fusion(bf16[32,384]{0,1:T(8,128)(2,1)S(1)} %bitcast.36, bf16[384,12288]{1,0:T(8,128)(2,1)} %param.4), kind=kOutput, calls=%fused_computation.36 | convolution fusion | flops 301989888 | bytes 11034624 | tf_op jit(solution)/shard_map/dot_general | solution.py:14
  29.8 0.0 reduce-scatter.2.cloned.1.call-update
  29.8 0.0 copy-done.1
  29.9 1.7 %reduce-window.6 = s32[16,6,128]{2,0,1:T(8,128)S(1)} reduce-window(s32[16,6,128]{2,0,1:T(8,128)S(1)} %fusion.11, s32[]{:T(128)} %constant.48.clone.1), window={size=1x1x128 pad=0_0x0_0x127_0}, to_apply=%region_1.2 | reduce-window | flops 1560576 | bytes 98308 | tf_op jit(solution)/shard_map/reduce-window
  31.6 0.3 slice_reduce_fusion
  31.9 0.1 fusion.8
  32.0 0.7 select_reduce_fusion
  32.7 0.7 convert_element_type.40
  33.4 10.3 %all-to-all-start.2 = ((f32[1,16,16]{2,0,1:T(1,128)}), f32[1,16,16]{2,0,1:T(1,128)S(1)}, u32[]{:S(2)}, u32[]{:S(2)}) async-start(f32[1,16,16]{2,0,1:T(1,128)} %convert_element_type.40), calls=%async_computation.3 | async-start | bytes 16384 | tf_op jit(solution)/shard_map/all_to_all | solution.py:43
  43.7 68.2 %reduce-scatter.2.cloned.1.call-done = f32[32,768]{1,0:T(8,128)} async-done(((f32[32,12288]{1,0:T(8,128)}), f32[32,768]{1,0:T(8,128)}) %reduce-scatter.2.cloned.1.call-update) | async-done | bytes 98320 | tf_op jit(solution)/shard_map/reduce_scatter | solution.py:22
  111.9 1.9 %fusion.1 = f32[32,256]{0,1:T(8,128)S(1)} fusion(f32[32,768]{1,0:T(8,128)} %reduce-scatter.2.cloned.1.call-done, s32[768]{0:T(1024)S(1)} %multiply_add_fusion, pred[768]{0:T(1024)(128)(4,1)S(1)} %get-tuple-element.6), kind=kOutput, calls=%fused_computation.5 | convolution fusion | flops 75890688 | bytes 134912 | tf_op jit(solution)/shard_map/dot_general | solution.py:35
  113.8 0.7 reshape.77
  114.5 0.0 all-to-all-done.2
  114.5 6.1 %all-to-all-start.1 = ((f32[16,1,512]{2,1,0:T(1,128)}), f32[16,1,512]{2,1,0:T(1,128)S(1)}, u32[]{:S(2)}, u32[]{:S(2)}) async-start(f32[16,1,512]{2,1,0:T(1,128)} %reshape.77), calls=%async_computation.2 | async-start | bytes 65536 | tf_op jit(solution)/shard_map/all_to_all | solution.py:42
  120.7 0.1 convert_element_type.42
  120.8 9.6 %all-to-all-done.1 = f32[16,1,512]{2,1,0:T(1,128)S(1)} async-done(((f32[16,1,512]{2,1,0:T(1,128)}), f32[16,1,512]{2,1,0:T(1,128)S(1)}, u32[]{:S(2)}, u32[]{:S(2)}) %all-to-all-start.1) | async-done | bytes 32800 | tf_op jit(solution)/shard_map/all_to_all | solution.py:42
  130.4 0.5 broadcast.62
  130.9 0.7 reduce.6
  131.6 0.1 reshape.78
  131.7 2.0 %convolution_add_fusion = f32[32,768]{1,0:T(8,128)} fusion(f32[32,256]{0,1:T(8,128)S(1)} %bitcast.37, s32[256]{0:T(256)S(1)} %convert_element_type.42, f32[32,768]{1,0:T(8,128)} %reduce-scatter.2.cloned.1.call-done, f32[768]{0:T(1024)S(1)} %get-tuple-element.5), kind=kOutput, calls=%fused_computation | convolution fusion | flops 75743232 | bytes 233472 | tf_op jit(solution)/shard_map/dot_general | solution.py:49
  (8 shorter events, 0.1 us)
Async XLA Ops:
  6.5 0.7 copy-start
  6.5 23.3 %copy-start.1 = (s32[768]{0:T(1024)S(1)}, s32[768]{0:T(1024)}, u32[]{:S(2)}) copy-start(s32[768]{0:T(1024)} %param.5) | copy-start | bytes 9220
  6.5 105.3 %reduce-scatter.2.cloned.1.call-start = ((), (), s32[]{:S(2)}) async-start(), calls=%async_computation.4 | async-start | bytes 1671168 | tf_op jit(solution)/shard_map/reduce_scatter | solution.py:22
  33.4 81.2 %all-to-all-start.2 = ((f32[1,16,16]{2,0,1:T(1,128)}), f32[1,16,16]{2,0,1:T(1,128)S(1)}, u32[]{:S(2)}, u32[]{:S(2)}) async-start(f32[1,16,16]{2,0,1:T(1,128)} %convert_element_type.40), calls=%async_computation.3 | async-start | bytes 16384 | tf_op jit(solution)/shard_map/all_to_all | solution.py:43
  114.5 15.9 %all-to-all-start.1 = ((f32[16,1,512]{2,1,0:T(1,128)}), f32[16,1,512]{2,1,0:T(1,128)S(1)}, u32[]{:S(2)}, u32[]{:S(2)}) async-start(f32[16,1,512]{2,1,0:T(1,128)} %reshape.77), calls=%async_computation.2 | async-start | bytes 65536 | tf_op jit(solution)/shard_map/all_to_all | solution.py:42
Sparse Core Ops, SparseCore 0:
  29.9 81.8 reduce-scatter.1
